TPU v7x, 32 devices: a whole 2x2x4 slice. The times are simulated.
32 devices in a mesh: space: 4 (over x, core), chan: 8 (over z, y).
Axes of the slice: x: 2, y: 2, z: 4, core: 2. Of those that a mesh axis runs over, the one named last changes fastest.
Arguments:
- inputs: bfloat16 [768, 64, 256], P('chan', 'space'), may hold values from -6 to 6
- initial_state: bfloat16 [384, 64, 256], P('chan', 'space'), may hold values from -6 to 6
- input_weight: bfloat16 [3, 9, 768, 384], P(None, None, 'chan'), may hold values from -0.0625 to 0.0625
- hidden_weight: bfloat16 [3, 9, 384, 384], P(None, None, 'chan'), may hold values from -0.0625 to 0.0625
- gate_bias: float32 [3, 384], replicated, may hold values from -3 to 3
Outputs:
- final_state: bfloat16 [384, 64, 256], P('chan', 'space')
All inputs are finite; a program needn't handle non-finite values.
Results may differ from a plain program's by a relative error of at most 0.0039.
Values may be sent and summed in bfloat16 or wider, within the bound.
A program may use at most 128 MiB of HBM per device.

v0:
```python
import jax
import jax.numpy as jnp
from jax import lax
from jax.sharding import PartitionSpec as P

STEPS = 2
OFFSETS = [(-1, -1), (-1, 0), (-1, 1), (0, -1), (0, 0), (0, 1), (1, -1), (1, 0), (1, 1)]


def extended(value, sides, width):
    for axis, dim in sides:
        count, length = (lax.axis_size(axis), value.shape[dim])
        up = [(i, (i + 1) % count) for i in range(count - 1)]
        down = [(j, i) for i, j in up]
        last = lax.slice_in_dim(value, length - width, length, axis=dim)
        initial = lax.slice_in_dim(value, 0, width, axis=dim)
        before = lax.ppermute(last, axis, up)
        after = lax.ppermute(initial, axis, down)
        value = jnp.concatenate([before, value, after], axis=dim)
    return value


def pad_columns(field):
    return jnp.pad(field, ((0, 0), (0, 0), (1, 1)))


def accumulate(total, padded, weight):
    heights = total.shape[2]
    widths = total.shape[3]
    for tap_index, (row_off, col_off) in enumerate(OFFSETS):
        window = padded[:, 1 + row_off : 1 + row_off + heights, 1 + col_off : 1 + col_off + widths]
        total = total + jnp.einsum(
            "gio,ihw->gohw", weight[:, tap_index], window, preferred_element_type=jnp.float32
        )
    return total


def folder(weight):

    def add_piece(total, piece, start):
        return accumulate(total, piece, weight)

    return add_piece


def per_device(inputs, initial_state, input_weight, hidden_weight, gate_bias):
    own_chan = initial_state.shape[0]
    band_rows = initial_state.shape[1]
    grid_cols = initial_state.shape[2]
    chan_rank = lax.axis_index("chan")
    input_own, hidden_own = (
        lax.all_to_all(input_weight, "chan", split_axis=3, concat_axis=2, tiled=True),
        lax.all_to_all(hidden_weight, "chan", split_axis=3, concat_axis=2, tiled=True),
    )
    input_padded = pad_columns(extended(inputs, (("space", 1),), 1))
    input_empty = jnp.zeros((3, own_chan, band_rows, grid_cols), jnp.float32)
    input_terms = folder(input_own)(
        input_empty, lax.all_gather(input_padded, "chan", axis=0, tiled=True), jnp.int32(0)
    )
    bias_own = lax.dynamic_slice_in_dim(gate_bias, chan_rank * own_chan, own_chan, 1)[
        :, :, None, None
    ]
    gate_fold = folder(hidden_own[0:2])
    cand_fold = folder(hidden_own[2:3])
    current = initial_state
    for repeat in range(STEPS):
        state_padded = pad_columns(extended(current, (("space", 1),), 1))
        gate_empty = jnp.zeros((2, own_chan, band_rows, grid_cols), jnp.float32)
        gate_pre = gate_fold(
            gate_empty, lax.all_gather(state_padded, "chan", axis=0, tiled=True), jnp.int32(0)
        )
        update = jax.nn.sigmoid(input_terms[0] + gate_pre[0] + bias_own[0])
        reset = jax.nn.sigmoid(input_terms[1] + gate_pre[1] + bias_own[1])
        gated = (reset * current.astype(jnp.float32)).astype(jnp.bfloat16)
        gated_padded = pad_columns(extended(gated, (("space", 1),), 1))
        cand_empty = jnp.zeros((1, own_chan, band_rows, grid_cols), jnp.float32)
        cand_pre = cand_fold(
            cand_empty, lax.all_gather(gated_padded, "chan", axis=0, tiled=True), jnp.int32(0)
        )
        candidate = jnp.tanh(input_terms[2] + cand_pre[0] + bias_own[2])
        current = ((1.0 - update) * current.astype(jnp.float32) + update * candidate).astype(
            jnp.bfloat16
        )
    return current


def solution(mesh):
    placed = (
        P("chan", "space", None),
        P("chan", "space", None),
        P(None, None, "chan", None),
        P(None, None, "chan", None),
        P(),
    )
    return jax.shard_map(
        per_device, mesh=mesh, in_specs=placed, out_specs=P("chan", "space", None), check_vma=False
    )
```

profile of v0, /device:TPU:0, one launch (start us, length us, event | category | flops | bytes accessed | tf_op | source)
XLA Modules:
  0.0 706.6 jit_solution(3591301017340858605)
XLA Ops:
  7.7 2.4 collective-permute-start.2
  11.5 3.9 collective-permute-done.3
  16.9 4.5 collective-permute-start
  22.7 1.8 collective-permute-done.1
  24.5 1.9 fusion.68
  26.4 4.6 copy.116
  31.0 8.2 %reshape.168 = bf16[8,2,31104]{2,1,0:T(2,128)(2,1)} reshape(bf16[384,3,9,48]{3,2,1,0:T(8,128)(2,1)} %bitcast.410) | data formatting | bytes 1990656
  39.2 5.8 all-to-all-start.1
  45.0 5.2 copy.109
  50.3 37.2 %all-to-all-done.1 = bf16[8,2,31104]{2,1,0:T(2,128)(2,1)S(1)} async-done(((bf16[8,2,31104]{2,1,0:T(2,128)(2,1)}), bf16[8,2,31104]{2,1,0:T(2,128)(2,1)S(1)}, u32[]{:S(2)}, u32[]{:S(2)}) %all-to-all-start.1) | async-done | bytes 995360 | tf_op jit(solution)/shard_map/all_to_all | solution.py:53
  88.5 5.9 all-to-all-start
  94.5 8.1 %reshape.169 = bf16[384,3,9,48]{3,2,1,0:T(8,128)(2,1)} reshape(bf16[8,2,31104]{2,1,0:T(2,128)(2,1)} %copy-done.5) | data formatting | bytes 1990656
  102.6 4.2 copy.182
  106.8 1.5 copy-done.4
  108.3 1.3 slice.435
  109.7 3.6 slice.340
  113.3 121.6 %all-to-all-done = bf16[3,9,96,384]{2,0,1,3:T(4,128)(2,1)S(1)} async-done(((bf16[3,9,96,384]{2,0,1,3:T(4,128)(2,1)}), bf16[3,9,96,384]{2,0,1,3:T(4,128)(2,1)S(1)}, u32[]{:S(2)}, u32[]{:S(2)}) %all-to-all-start) | async-done | bytes 1990688 | tf_op jit(solution)/shard_map/all_to_all | solution.py:52
  236.2 3.3 all_to_all.27
  239.6 4.6 fusion.55
  244.2 2.6 fusion.56
  253.2 3.1 add_bitcast_fusion.2
  256.3 74.9 %all-gather.6.cloned.1.call-done = bf16[768,18,258]{2,0,1:T(8,128)(2,1)} async-done(((bf16[96,18,258]{2,0,1:T(8,128)(2,1)}), bf16[768,18,258]{2,0,1:T(8,128)(2,1)}) %all-gather.6.cloned.1.call-update) | async-done | bytes 7133200 | tf_op jit(solution)/shard_map/all_gather | solution.py:58
  331.2 6.6 fusion.1
  337.8 5.6 fusion.2
  343.4 3.8 fusion.3
  347.2 3.8 fusion.4
  350.9 2.6 fusion.5
  353.5 3.8 fusion.6
  357.3 4.0 fusion.7
  361.2 2.6 fusion.8
  363.8 7.9 %add_bitcast_fusion = f32[3,48,16,256]{3,1,0,2:T(8,128)S(1)} fusion(f32[16,256,3,48]{1,3,2,0:T(8,128)S(1)} %fusion.1, f32[16,256,3,48]{1,3,2,0:T(8,128)} %fusion.2, f32[16,256,3,48]{1,3,2,0:T(8,128)} %fusion.3, f32[16,256,3,48]{1,3,2,0:T(8,128)} %fusion.4, f32[16,256,3,48]{1,3,2,0:T(8,128)} %fusion.5, f32[16,256,3,48]{1,3,2,0:T(8,128)} %fusion.6, ...), kind=kOutput, calls=%fused_computation.94 | convolution fusion | flops 910688256 | bytes 27746304 | tf_op jit(solution)/shard_map/gio,ihw->gohw/dot_general | solution.py:32
  374.7 3.5 collective-permute-done.5
  380.8 1.3 slice.368
  382.1 83.5 %all-gather.10.cloned.1.call-done = bf16[384,18,258]{2,0,1:T(8,128)(2,1)} async-done(((bf16[48,18,258]{2,0,1:T(8,128)(2,1)}), bf16[384,18,258]{2,0,1:T(8,128)(2,1)}) %all-gather.10.cloned.1.call-update) | async-done | bytes 3566608 | tf_op jit(solution)/shard_map/all_gather | solution.py:78
  465.6 3.6 fusion.50
  469.2 3.4 fusion.48
  478.9 1.6 fusion.154
  483.1 3.5 collective-permute-done.7
  488.0 86.1 %all-gather.12.cloned.1.call-done = bf16[384,18,258]{2,0,1:T(8,128)(2,1)} async-done(((bf16[48,18,258]{2,0,1:T(8,128)(2,1)}), bf16[384,18,258]{2,0,1:T(8,128)(2,1)}) %all-gather.12.cloned.1.call-update) | async-done | bytes 3566608 | tf_op jit(solution)/shard_map/all_gather | solution.py:70
  574.2 3.7 fusion.34
  577.9 2.6 fusion.35
  587.0 1.9 add_bitcast_fusion.1
  591.7 1.5 collective-permute-start.9
  593.2 3.2 collective-permute-done.9
  597.7 86.4 %all-gather.14.cloned.1.call-done = bf16[384,18,258]{2,0,1:T(8,128)(2,1)} async-done(((bf16[48,18,258]{2,0,1:T(8,128)(2,1)}), bf16[384,18,258]{2,0,1:T(8,128)(2,1)}) %all-gather.14.cloned.1.call-update) | async-done | bytes 3566608 | tf_op jit(solution)/shard_map/all_gather | solution.py:78
  684.1 3.6 fusion.23
  687.7 3.4 fusion.21
  697.3 1.5 fusion.157
  (114 shorter events, 47.2 us)
Async XLA Ops:
  6.5 87.9 %copy-start = (f32[3,384]{1,0:T(4,128)S(1)}, f32[3,384]{1,0:T(4,128)}, u32[]{:S(2)}) copy-start(f32[3,384]{1,0:T(4,128)} %param.9) | copy-start | bytes 13828
  6.5 10.1 %copy-start.20 = (bf16[96,16,256]{2,1,0:T(8,128)(2,1)S(1)}, bf16[96,16,256]{2,1,0:T(8,128)(2,1)}, u32[]{:S(2)}) copy-start(bf16[96,16,256]{2,1,0:T(8,128)(2,1)} %param.5) | copy-start | bytes 2359300
  6.5 233.0 %all-gather.8.cloned.1.call-start = ((), (), s32[]{:S(2)}) async-start(), calls=%async_computation.3 | async-start | bytes 5971968 | tf_op jit(solution)/shard_map/all_gather | solution.py:70
  7.7 3.7 collective-permute-start.2
  10.2 5.2 collective-permute-start.3
  16.5 9.9 %copy-start.17 = (bf16[3,9,48,384]{3,2,1,0:T(8,128)(2,1)S(1)}, bf16[3,9,48,384]{3,2,1,0:T(8,128)(2,1)}, u32[]{:S(2)}) copy-start(bf16[3,9,48,384]{3,2,1,0:T(8,128)(2,1)} %param.8) | copy-start | bytes 2985988
  16.5 314.6 %all-gather.6.cloned.1.call-start = ((), (), s32[]{:S(2)}) async-start(), calls=%async_computation.2 | async-start | bytes 11943936 | tf_op jit(solution)/shard_map/all_gather | solution.py:58
  16.9 5.8 collective-permute-start
  21.3 3.1 collective-permute-start.1
  31.0 14.1 %copy-start.12 = (bf16[3,9,96,384]{3,2,1,0:T(8,128)(2,1)S(1)}, bf16[3,9,96,384]{3,2,1,0:T(8,128)(2,1)}, u32[]{:S(2)}) copy-start(bf16[3,9,96,384]{3,2,1,0:T(8,128)(2,1)} %param.7) | copy-start | bytes 5971972
  39.2 48.3 %all-to-all-start.1 = ((bf16[8,2,31104]{2,1,0:T(2,128)(2,1)}), bf16[8,2,31104]{2,1,0:T(2,128)(2,1)S(1)}, u32[]{:S(2)}, u32[]{:S(2)}) async-start(bf16[8,2,31104]{2,1,0:T(2,128)(2,1)} %reshape.168), calls=%async_computation.1 | async-start | bytes 1990656 | tf_op jit(solution)/shard_map/all_to_all | solution.py:53
  87.5 1.0 copy-start.5
  88.5 146.4 %all-to-all-start = ((bf16[3,9,96,384]{2,0,1,3:T(4,128)(2,1)}), bf16[3,9,96,384]{2,0,1,3:T(4,128)(2,1)S(1)}, u32[]{:S(2)}, u32[]{:S(2)}) async-start(bf16[3,9,96,384]{2,0,1,3:T(4,128)(2,1)} %copy.109), calls=%async_computation | async-start | bytes 7077888 | tf_op jit(solution)/shard_map/all_to_all | solution.py:52
  94.4 371.2 %all-gather.10.cloned.1.call-start = ((), (), s32[]{:S(2)}) async-start(), calls=%async_computation.4 | async-start | bytes 5971968 | tf_op jit(solution)/shard_map/all_gather | solution.py:78
  106.8 1.5 copy-start.4
  236.2 3.4 copy-start.18
  239.6 7.2 %copy-start.13 = (bf16[384,18,258]{2,0,1:T(8,128)(2,1)S(1)}, bf16[384,18,258]{2,0,1:T(8,128)(2,1)}, u32[]{:S(2)}) copy-start(bf16[384,18,258]{2,0,1:T(8,128)(2,1)} %all-gather.8.cloned.1.call-done) | copy-start | bytes 10699780
  253.2 78.0 %copy-start.11 = (bf16[3,9,768,48]{2,3,0,1:T(8,128)(2,1)S(1)}, bf16[3,9,768,48]{2,3,0,1:T(8,128)(2,1)}, u32[]{:S(2)}) copy-start(bf16[3,9,768,48]{2,3,0,1:T(8,128)(2,1)} %all_to_all.27) | copy-start | bytes 5971972
  331.2 12.2 %slice-start = ((s8[10616832]{0:T(1024)(128)(4,1)}), s8[4194304]{0:T(1024)(128)(4,1)S(1)}, s32[]{:S(2)}) async-start(s8[10616832]{0:T(1024)(128)(4,1)} %bitcast.414), calls=%async_computation.7 | async-start | bytes 8388608
  331.2 12.2 %slice-start.1 = ((s8[10616832]{0:T(1024)(128)(4,1)}), s8[4194304]{0:T(1024)(128)(4,1)S(1)}, s32[]{:S(2)}) async-start(s8[10616832]{0:T(1024)(128)(4,1)} %bitcast.414), calls=%async_computation.8 | async-start | bytes 8388608
  337.8 5.6 slice-start.2
  363.8 7.9 %copy-start.6 = (f32[2,48,16,256]{3,1,2,0:T(8,128)S(1)}, f32[2,48,16,256]{3,1,2,0:T(8,128)}, u32[]{:S(2)}) copy-start(f32[2,48,16,256]{3,1,2,0:T(8,128)} %add_bitcast_fusion.2) | copy-start | bytes 4718596
  363.8 7.9 %copy-start.15 = (bf16[48,16,256]{2,1,0:T(8,128)(2,1)S(1)}, bf16[48,16,256]{2,1,0:T(8,128)(2,1)}, u32[]{:S(2)}) copy-start(bf16[48,16,256]{2,1,0:T(8,128)(2,1)} %param.6) | copy-start | bytes 1179652
  372.1 2.6 collective-permute-start.4
  373.4 4.8 collective-permute-start.5
  379.5 194.7 %all-gather.12.cloned.1.call-start = ((), (), s32[]{:S(2)}) async-start(), calls=%async_computation.5 | async-start | bytes 5971968 | tf_op jit(solution)/shard_map/all_gather | solution.py:70
  382.1 87.1 %copy-start.10 = (bf16[1,9,384,48]{2,3,1,0:T(8,128)(2,1)S(1)}, bf16[1,9,384,48]{2,3,1,0:T(8,128)(2,1)}, u32[]{:S(2)}) copy-start(bf16[1,9,384,48]{2,3,1,0:T(8,128)(2,1)} %slice.368) | copy-start | bytes 995332
  465.6 7.1 %copy-start.2 = (bf16[384,18,258]{2,0,1:T(8,128)(2,1)S(1)}, bf16[384,18,258]{2,0,1:T(8,128)(2,1)}, u32[]{:S(2)}) copy-start(bf16[384,18,258]{2,0,1:T(8,128)(2,1)} %all-gather.10.cloned.1.call-done) | copy-start | bytes 10699780
  477.4 1.4 copy-start.7
  477.4 1.5 copy-start.16
  480.5 2.6 collective-permute-start.6
  481.8 4.8 collective-permute-start.7
  487.8 196.3 %all-gather.14.cloned.1.call-start = ((), (), s32[]{:S(2)}) async-start(), calls=%async_computation.6 | async-start | bytes 5971968 | tf_op jit(solution)/shard_map/all_gather | solution.py:78
  574.2 6.4 copy-start.14
  577.9 2.7 copy-start.19
  588.9 1.2 copy-start.8
  590.4 2.9 collective-permute-start.8
  591.7 4.8 collective-permute-start.9
  684.1 7.1 copy-start.3
  695.8 1.4 copy-start.9
  695.9 3.8 copy-start.1
Sparse Core Ops, SparseCore 0:
  16.7 123.2 all-gather.7
  142.2 188.9 all-gather.5
  379.6 85.9 all-gather.9
  487.9 86.2 all-gather.11
  597.8 86.2 all-gather.13
where the time goes:
time: 714 us; the launch traced here: 707 us
  waiting for transfers between devices  506 us (71%)
  matrix products  99.9 us (14%)
  local copies, waits for them, and re-layouts  49.9 us (7%)
  starting transfers between devices  29.6 us (4%)
  between operations  14.2 us (2%)
  other arithmetic  7.41 us (1%)
    all_gather x2, waiting for transfers between devices, per_device(): lax.all_gather(gated_padded, 'chan', axis=0, tiled=True)  170 us
    all_to_all x1, waiting for transfers between devices, per_device(): lax.all_to_all(input_weight, 'chan', split_axis=3, concat_axis=2, tiled=T...  122 us
    dot_general x45, matrix products, accumulate(): jnp.einsum('gio,ihw->gohw', weight[:, tap_index], window, preferred_eleme...  99.9 us
    all_gather x2, waiting for transfers between devices, per_device(): lax.all_gather(state_padded, 'chan', axis=0, tiled=True)  86.1 us
    all_gather x1, waiting for transfers between devices, per_device(): lax.all_gather(input_padded, 'chan', axis=0, tiled=True)  74.9 us
    all_to_all x1, waiting for transfers between devices, per_device(): lax.all_to_all(hidden_weight, 'chan', split_axis=3, concat_axis=2, tiled=...  37.2 us
    unnamed x54, local copies, waits for them, and re-layouts  32.5 us
    ppermute x5, waiting for transfers between devices, extended(): after = lax.ppermute(initial, axis, down)  15.9 us
  transfers between devices with their start and end apart: 17, of which 11 were waited for; matrix products, arithmetic and copies ran while one was open for 8% of the time, Pallas kernels for 0%

commit v1 on v0

--- a/solution.py
+++ b/solution.py
@@ -75,7 +75,12 @@
         gated_padded = pad_columns(extended(gated, (("space", 1),), 1))
         cand_empty = jnp.zeros((1, own_chan, band_rows, grid_cols), jnp.float32)
         cand_pre = cand_fold(
-            cand_empty, lax.all_gather(gated_padded, "chan", axis=0, tiled=True), jnp.int32(0)
+            cand_empty,
+            jnp.concatenate(
+                lax.all_to_all(jnp.stack([gated_padded] * lax.axis_size("chan")), "chan", 0, 0),
+                axis=0,
+            ),
+            jnp.int32(0),
         )
         candidate = jnp.tanh(input_terms[2] + cand_pre[0] + bias_own[2])
         current = ((1.0 - update) * current.astype(jnp.float32) + update * candidate).astype(

time: 714 us -> 779 us (1.091)
  blocking collectives: 0 us -> 121 us
  waiting for transfers between devices: 506 us -> 449 us
  matrix products: 99.9 us -> 89.7 us
    all_gather x2 -> x0, waiting for transfers between devices: 170 us -> none  [per_device(): lax.all_gather(gated_padded, 'chan', axis=0, tiled=True)]
    all_to_all x0 -> x1, blocking collectives: none -> 121 us  [per_device(): lax.all_to_all(jnp.stack([gated_padded] * lax.axis_size('chan')), 'chan',...]
    all_to_all x0 -> x1, waiting for transfers between devices: none -> 115 us  [per_device(): lax.all_to_all(jnp.stack([gated_padded] * lax.axis_size('chan')), 'chan',...]
    dot_general x45, matrix products: 99.9 us -> 89.7 us  [accumulate(): jnp.einsum('gio,ihw->gohw', weight[:, tap_index], window, preferred_eleme...]
    unnamed x54 -> x46, local copies, waits for them, and re-layouts: 32.5 us -> 30.8 us
  transfers between devices with their start and end apart: 17 -> 16, of which waited for: 11 -> 10; matrix products, arithmetic and copies ran while one was open for 8% -> 7% of each run, Pallas kernels for 0% -> 0%
where the time goes in v1:
time: 779 us; the launch traced here: 771 us
  waiting for transfers between devices  449 us (58%)
  blocking collectives  121 us (16%)
  matrix products  89.7 us (12%)
  local copies, waits for them, and re-layouts  55.7 us (7%)
  starting transfers between devices  35.9 us (5%)
  between operations  14.2 us (2%)
    all_to_all x1, waiting for transfers between devices, per_device(): lax.all_to_all(input_weight, 'chan', split_axis=3, concat_axis=2, tiled=T...  122 us
    all_to_all x1, blocking collectives, per_device(): lax.all_to_all(jnp.stack([gated_padded] * lax.axis_size('chan')), 'chan',...  121 us
    all_to_all x1, waiting for transfers between devices, per_device(): lax.all_to_all(jnp.stack([gated_padded] * lax.axis_size('chan')), 'chan',...  115 us
    dot_general x45, matrix products, accumulate(): jnp.einsum('gio,ihw->gohw', weight[:, tap_index], window, preferred_eleme...  89.7 us
    all_gather x2, waiting for transfers between devices, per_device(): lax.all_gather(state_padded, 'chan', axis=0, tiled=True)  86.3 us
    all_gather x1, waiting for transfers between devices, per_device(): lax.all_gather(input_padded, 'chan', axis=0, tiled=True)  74.3 us
    all_to_all x1, waiting for transfers between devices, per_device(): lax.all_to_all(hidden_weight, 'chan', split_axis=3, concat_axis=2, tiled=...  37.2 us
    unnamed x46, local copies, waits for them, and re-layouts  30.8 us
  transfers between devices with their start and end apart: 16, of which 10 were waited for; matrix products, arithmetic and copies ran while one was open for 7% of the time, Pallas kernels for 0%

profile of v1, /device:TPU:0, one launch (start us, length us, event | category | flops | bytes accessed | tf_op | source)
XLA Modules:
  0.0 771.2 jit_solution(15794956840456651753)
XLA Ops:
  7.7 2.4 collective-permute-start.2
  11.5 3.9 collective-permute-done.3
  16.9 4.5 collective-permute-start
  22.6 1.8 collective-permute-done.1
  24.5 1.9 fusion.68
  26.4 4.6 copy.118
  31.0 8.2 %reshape.180 = bf16[8,2,31104]{2,1,0:T(2,128)(2,1)} reshape(bf16[384,3,9,48]{3,2,1,0:T(8,128)(2,1)} %bitcast.430) | data formatting | bytes 1990656
  39.2 5.8 all-to-all-start.1
  45.1 5.2 copy.111
  50.3 37.2 %all-to-all-done.1 = bf16[8,2,31104]{2,1,0:T(2,128)(2,1)S(1)} async-done(((bf16[8,2,31104]{2,1,0:T(2,128)(2,1)}), bf16[8,2,31104]{2,1,0:T(2,128)(2,1)S(1)}, u32[]{:S(2)}, u32[]{:S(2)}) %all-to-all-start.1) | async-done | bytes 995360 | tf_op jit(solution)/shard_map/all_to_all | solution.py:53
  88.5 5.9 all-to-all-start
  94.5 8.1 %reshape.181 = bf16[384,3,9,48]{3,2,1,0:T(8,128)(2,1)} reshape(bf16[8,2,31104]{2,1,0:T(2,128)(2,1)} %copy-done.3) | data formatting | bytes 1990656
  102.6 4.2 copy.186
  106.8 1.5 copy-done.2
  108.3 1.3 slice.435
  109.6 3.6 slice.340
  113.3 122.4 %all-to-all-done = bf16[3,9,96,384]{2,0,1,3:T(4,128)(2,1)S(1)} async-done(((bf16[3,9,96,384]{2,0,1,3:T(4,128)(2,1)}), bf16[3,9,96,384]{2,0,1,3:T(4,128)(2,1)S(1)}, u32[]{:S(2)}, u32[]{:S(2)}) %all-to-all-start) | async-done | bytes 1990688 | tf_op jit(solution)/shard_map/all_to_all | solution.py:52
  237.0 3.3 all_to_all.33
  240.4 4.3 fusion.55
  244.7 2.6 fusion.56
  253.7 3.0 add_bitcast_fusion.2
  256.8 74.3 %all-gather.4.cloned.1.call-done = bf16[768,18,258]{2,0,1:T(8,128)(2,1)} async-done(((bf16[96,18,258]{2,0,1:T(8,128)(2,1)}), bf16[768,18,258]{2,0,1:T(8,128)(2,1)}) %all-gather.4.cloned.1.call-update) | async-done | bytes 7133200 | tf_op jit(solution)/shard_map/all_gather | solution.py:58
  331.1 6.6 fusion.1
  337.7 5.6 fusion.2
  343.3 3.8 fusion.3
  347.1 3.8 fusion.4
  350.9 2.5 fusion.5
  353.4 3.7 fusion.6
  357.1 3.9 fusion.7
  361.1 2.6 fusion.8
  363.7 7.9 %add_bitcast_fusion = f32[3,48,16,256]{3,1,0,2:T(8,128)S(1)} fusion(f32[16,256,3,48]{1,3,2,0:T(8,128)S(1)} %fusion.1, f32[16,256,3,48]{1,3,2,0:T(8,128)} %fusion.2, f32[16,256,3,48]{1,3,2,0:T(8,128)} %fusion.3, f32[16,256,3,48]{1,3,2,0:T(8,128)} %fusion.4, f32[16,256,3,48]{1,3,2,0:T(8,128)} %fusion.5, f32[16,256,3,48]{1,3,2,0:T(8,128)} %fusion.6, ...), kind=kOutput, calls=%fused_computation.94 | convolution fusion | flops 910688256 | bytes 27746304 | tf_op jit(solution)/shard_map/gio,ihw->gohw/dot_general | solution.py:32
  374.6 3.5 collective-permute-done.5
  378.4 2.9 stack.4
  381.3 4.7 all-to-all-start.2
  387.2 1.3 slice.368
  388.6 114.7 %all-to-all-done.2 = bf16[8,48,18,258]{3,1,2,0:T(8,128)(2,1)} async-done(((bf16[8,48,18,258]{3,1,2,0:T(8,128)(2,1)}), bf16[8,48,18,258]{3,1,2,0:T(8,128)(2,1)}, u32[]{:S(2)}, u32[]{:S(2)}) %all-to-all-start.2) | async-done | bytes 3566624 | tf_op jit(solution)/shard_map/all_to_all | solution.py:80
  503.3 3.3 copy.132
  516.5 3.3 collective-permute-start.6
  519.8 1.5 collective-permute-start.7
  521.3 1.6 collective-permute-done.7
  524.1 86.2 %all-gather.8.cloned.1.call-done = bf16[384,18,258]{2,0,1:T(8,128)(2,1)} async-done(((bf16[48,18,258]{2,0,1:T(8,128)(2,1)}), bf16[384,18,258]{2,0,1:T(8,128)(2,1)}) %all-gather.8.cloned.1.call-update) | async-done | bytes 3566608 | tf_op jit(solution)/shard_map/all_gather | solution.py:70
  610.3 3.7 fusion.34
  614.1 2.6 fusion.35
  620.0 1.3 fusion.30
  622.0 1.3 fusion.28
  623.4 1.9 add_bitcast_fusion.1
  628.2 3.5 collective-permute-done.9
  632.5 120.9 %all_to_all.43 = bf16[8,48,18,258]{3,1,2,0:T(8,128)(2,1)S(1)} all-to-all(bf16[8,48,18,258]{3,1,2,0:T(8,128)(2,1)S(1)} %stack.5), channel_id=1, replica_groups=mesh['space'=4,'chan'=8] {'chan'}, dimensions={0} | all-to-all | bytes 7133184 | tf_op jit(solution)/shard_map/all_to_all | solution.py:80
  (107 shorter events, 48.1 us)
Async XLA Ops:
  6.5 87.9 %copy-start = (f32[3,384]{1,0:T(4,128)S(1)}, f32[3,384]{1,0:T(4,128)}, u32[]{:S(2)}) copy-start(f32[3,384]{1,0:T(4,128)} %param.9) | copy-start | bytes 13828
  6.5 10.0 %copy-start.16 = (bf16[96,16,256]{2,1,0:T(8,128)(2,1)S(1)}, bf16[96,16,256]{2,1,0:T(8,128)(2,1)}, u32[]{:S(2)}) copy-start(bf16[96,16,256]{2,1,0:T(8,128)(2,1)} %param.5) | copy-start | bytes 2359300
  6.5 233.9 %all-gather.6.cloned.1.call-start = ((), (), s32[]{:S(2)}) async-start(), calls=%async_computation.5 | async-start | bytes 5971968 | tf_op jit(solution)/shard_map/all_gather | solution.py:70
  7.7 3.7 collective-permute-start.2
  10.2 5.2 collective-permute-start.3
  16.5 9.9 %copy-start.13 = (bf16[3,9,48,384]{3,2,1,0:T(8,128)(2,1)S(1)}, bf16[3,9,48,384]{3,2,1,0:T(8,128)(2,1)}, u32[]{:S(2)}) copy-start(bf16[3,9,48,384]{3,2,1,0:T(8,128)(2,1)} %param.8) | copy-start | bytes 2985988
  16.5 314.5 %all-gather.4.cloned.1.call-start = ((), (), s32[]{:S(2)}) async-start(), calls=%async_computation.4 | async-start | bytes 11943936 | tf_op jit(solution)/shard_map/all_gather | solution.py:58
  16.9 5.8 collective-permute-start
  21.3 3.1 collective-permute-start.1
  31.0 14.1 %copy-start.8 = (bf16[3,9,96,384]{3,2,1,0:T(8,128)(2,1)S(1)}, bf16[3,9,96,384]{3,2,1,0:T(8,128)(2,1)}, u32[]{:S(2)}) copy-start(bf16[3,9,96,384]{3,2,1,0:T(8,128)(2,1)} %param.7) | copy-start | bytes 5971972
  39.2 48.3 %all-to-all-start.1 = ((bf16[8,2,31104]{2,1,0:T(2,128)(2,1)}), bf16[8,2,31104]{2,1,0:T(2,128)(2,1)S(1)}, u32[]{:S(2)}, u32[]{:S(2)}) async-start(bf16[8,2,31104]{2,1,0:T(2,128)(2,1)} %reshape.180), calls=%async_computation.1 | async-start | bytes 1990656 | tf_op jit(solution)/shard_map/all_to_all | solution.py:53
  87.5 1.0 copy-start.3
  88.5 147.2 %all-to-all-start = ((bf16[3,9,96,384]{2,0,1,3:T(4,128)(2,1)}), bf16[3,9,96,384]{2,0,1,3:T(4,128)(2,1)S(1)}, u32[]{:S(2)}, u32[]{:S(2)}) async-start(bf16[3,9,96,384]{2,0,1,3:T(4,128)(2,1)} %copy.111), calls=%async_computation | async-start | bytes 7077888 | tf_op jit(solution)/shard_map/all_to_all | solution.py:52
  106.8 1.5 copy-start.2
  237.0 3.4 copy-start.14
  240.4 6.8 copy-start.9
  253.7 77.4 %copy-start.7 = (bf16[3,9,768,48]{2,3,0,1:T(8,128)(2,1)S(1)}, bf16[3,9,768,48]{2,3,0,1:T(8,128)(2,1)}, u32[]{:S(2)}) copy-start(bf16[3,9,768,48]{2,3,0,1:T(8,128)(2,1)} %all_to_all.33) | copy-start | bytes 5971972
  331.1 12.2 %slice-start = ((s8[10616832]{0:T(1024)(128)(4,1)}), s8[4194304]{0:T(1024)(128)(4,1)S(1)}, s32[]{:S(2)}) async-start(s8[10616832]{0:T(1024)(128)(4,1)} %bitcast.434), calls=%async_computation.7 | async-start | bytes 8388608
  331.1 12.2 %slice-start.1 = ((s8[10616832]{0:T(1024)(128)(4,1)}), s8[4194304]{0:T(1024)(128)(4,1)S(1)}, s32[]{:S(2)}) async-start(s8[10616832]{0:T(1024)(128)(4,1)} %bitcast.434), calls=%async_computation.8 | async-start | bytes 8388608
  337.7 5.6 slice-start.2
  363.7 7.9 %copy-start.4 = (f32[2,48,16,256]{3,1,2,0:T(8,128)S(1)}, f32[2,48,16,256]{3,1,2,0:T(8,128)}, u32[]{:S(2)}) copy-start(f32[2,48,16,256]{3,1,2,0:T(8,128)} %add_bitcast_fusion.2) | copy-start | bytes 4718596
  363.7 7.9 %copy-start.11 = (bf16[48,16,256]{2,1,0:T(8,128)(2,1)S(1)}, bf16[48,16,256]{2,1,0:T(8,128)(2,1)}, u32[]{:S(2)}) copy-start(bf16[48,16,256]{2,1,0:T(8,128)(2,1)} %param.6) | copy-start | bytes 1179652
  372.0 2.6 collective-permute-start.4
  373.3 4.8 collective-permute-start.5
  381.3 122.0 %all-to-all-start.2 = ((bf16[8,48,18,258]{3,1,2,0:T(8,128)(2,1)}), bf16[8,48,18,258]{3,1,2,0:T(8,128)(2,1)}, u32[]{:S(2)}, u32[]{:S(2)}) async-start(bf16[8,48,18,258]{3,1,2,0:T(8,128)(2,1)} %stack.4), calls=%async_computation.2 | async-start | bytes 10616832 | tf_op jit(solution)/shard_map/all_to_all | solution.py:80
  386.0 224.4 %all-gather.8.cloned.1.call-start = ((), (), s32[]{:S(2)}) async-start(), calls=%async_computation.6 | async-start | bytes 5971968 | tf_op jit(solution)/shard_map/all_gather | solution.py:70
  388.6 118.1 %copy-start.6 = (bf16[1,9,384,48]{2,3,1,0:T(8,128)(2,1)S(1)}, bf16[1,9,384,48]{2,3,1,0:T(8,128)(2,1)}, u32[]{:S(2)}) copy-start(bf16[1,9,384,48]{2,3,1,0:T(8,128)(2,1)} %slice.368) | copy-start | bytes 995332
  514.0 1.4 copy-start.5
  514.0 1.5 copy-start.12
  516.5 4.8 collective-permute-start.6
  519.8 3.1 collective-permute-start.7
  610.3 6.4 copy-start.10
  614.1 2.7 copy-start.15
  625.6 2.6 collective-permute-start.8
  626.9 4.8 collective-permute-start.9
  761.6 2.6 copy-start.1
Sparse Core Ops, SparseCore 0:
  16.7 123.0 all-gather.5
  141.9 189.0 all-gather.3
  524.2 86.0 all-gather.7
